TPU v7x, 256 devices: a whole 4x4x8 slice. The times are simulated.
256 devices in a mesh: tp: 4 (over z_lo), sy: 8 (over x, core), sx: 8 (over y, z_hi).
Axes of the slice: x: 4, y: 4, z: 8 (z_hi: 2, z_lo: 4; z = z_hi * 4 + z_lo), core: 2. Of those that a mesh axis runs over, the one named last changes fastest.
Arguments:
- queries: bfloat16 [24, 4, 64, 64, 128], P('tp', None, 'sy', 'sx'), may hold values from -8 to 8
- key_vectors: bfloat16 [24, 4, 64, 64, 128], P('tp', None, 'sy', 'sx'), may hold values from -8 to 8
- value_vectors: bfloat16 [24, 4, 64, 64, 128], P('tp', None, 'sy', 'sx'), may hold values from -6 to 6
- out_grad: bfloat16 [24, 4, 64, 64, 128], P('tp', None, 'sy', 'sx'), may hold values from -6 to 6
- cell_valid: int32 [64, 64], replicated, may hold values from 0 to 1, as said below
Outputs:
- query_grad: bfloat16 [24, 4, 64, 64, 128], P('tp', None, 'sy', 'sx')
- key_grad: bfloat16 [24, 4, 64, 64, 128], P('tp', None, 'sy', 'sx')
- value_grad: bfloat16 [24, 4, 64, 64, 128], P('tp', None, 'sy', 'sx')
Inputs may be any that keep to these rules, and one draw needn't show every extreme that they name: cell_valid is 1 exactly on one rectangle of cells and 0 elsewhere; the rectangle holds the rows 16 to 59 and the columns 16 to 59.
All inputs are finite; a program needn't handle non-finite values.
Results may differ from a plain program's by a relative error of at most 0.0085.
Values may be sent and summed in bfloat16 or wider, within the bound.
A program may use at most 64 MiB of HBM per device.

v0:
```python
import math

import jax
import jax.numpy as jnp
from jax import lax
from jax.sharding import PartitionSpec as P


def extended(block, sides, width):
    for axis, dim in sides:
        count = lax.axis_size(axis)
        forward = [(i, i + 1) for i in range(count - 1)]
        backward = [(target, source) for source, target in forward]
        low = lax.ppermute(
            lax.slice_in_dim(block, block.shape[dim] - width, None, axis=dim), axis, forward
        )
        high = lax.ppermute(lax.slice_in_dim(block, 0, width, axis=dim), axis, backward)
        block = jnp.concatenate([low, block, high], axis=dim)
    return block


def passed_along(block, axis, distance):
    devices = range(lax.axis_size(axis))
    route = [(i - distance, i) for i in devices if i - distance in devices]
    return lax.ppermute(block, axis, route)


def window_mask(cell_rim, frames, tile_size):
    rim_span = 3 * tile_size
    offset = jnp.arange(rim_span)[None, :] - tile_size - jnp.arange(tile_size)[:, None]
    inside = jnp.abs(offset) <= tile_size
    key_ok = cell_rim == 1
    query_ok = key_ok[tile_size : 2 * tile_size, tile_size : 2 * tile_size]
    cell_pairs = (
        inside[:, None, :, None]
        & inside[None, :, None, :]
        & key_ok[None, None]
        & query_ok[:, :, None, None]
    )
    allowed = jnp.broadcast_to(
        cell_pairs[None, :, :, None], (frames, tile_size, tile_size, frames, rim_span, rim_span)
    )
    allowed = allowed.reshape(frames * tile_size * tile_size, frames * rim_span * rim_span)
    query_live = jnp.broadcast_to(query_ok[None], (frames, tile_size, tile_size)).reshape(-1)
    return (allowed, query_live)


def contract_last(left_rows, right_rows):
    return lax.dot_general(
        left_rows, right_rows, (((1,), (1,)), ((), ())), preferred_element_type=jnp.float32
    )


def contract_first(left_rows, right_rows):
    return lax.dot_general(
        left_rows, right_rows, (((0,), (0,)), ((), ())), preferred_element_type=jnp.float32
    )


def query_pass(query_rows, grad_rows, key_rows, value_rows, allowed, query_live, score_scale):
    scores = contract_last(query_rows, key_rows) * score_scale
    masked = jnp.where(allowed, scores, -jnp.inf)
    row_max = jnp.where(query_live, jnp.max(masked, axis=1), 0.0)
    unnormed = jnp.where(allowed, jnp.exp(scores - row_max[:, None]), 0.0)
    row_total = jnp.sum(unnormed, axis=1) + jnp.where(query_live, 0.0, 1.0)
    probs = unnormed / row_total[:, None]
    probs_low = probs.astype(jnp.bfloat16)
    attended = jnp.dot(probs_low, value_rows, preferred_element_type=jnp.float32)
    row_delta = jnp.sum(grad_rows.astype(jnp.float32) * attended, axis=1)
    dprobs = contract_last(grad_rows, value_rows)
    dscores_low = (probs * (dprobs - row_delta[:, None])).astype(jnp.bfloat16)
    query_part = jnp.dot(dscores_low, key_rows, preferred_element_type=jnp.float32) * score_scale
    return (probs_low, dscores_low, query_part, row_max, row_total, row_delta)


def local(queries, key_vectors, value_vectors, out_grad, cell_valid):
    tile_size = queries.shape[2]
    frames = queries.shape[1]
    width = queries.shape[-1]
    score_scale = 1.0 / math.sqrt(width)
    row_place = lax.axis_index("sy") * tile_size
    column_place = lax.axis_index("sx") * tile_size
    cell_rim = lax.dynamic_slice(
        jnp.pad(cell_valid, tile_size), (row_place, column_place), (3 * tile_size, 3 * tile_size)
    )
    allowed, query_live = window_mask(cell_rim, frames, tile_size)
    pair_local = jnp.stack([key_vectors, value_vectors], 1)
    pair_rims = extended(pair_local, (("sy", 3), ("sx", 4)), tile_size)

    def head_returned(inputs):
        query_head, grad_head, pair_rim = inputs
        query_rows = query_head.reshape(-1, width)
        grad_rows = grad_head.reshape(-1, width)
        probs_low, dscores_low, query_part, row_max, row_total, row_delta = query_pass(
            query_rows,
            grad_rows,
            pair_rim[0].reshape(-1, width),
            pair_rim[1].reshape(-1, width),
            allowed,
            query_live,
            score_scale,
        )
        key_part = (contract_first(dscores_low, query_rows) * score_scale).astype(jnp.bfloat16)
        value_part = contract_first(probs_low, grad_rows).astype(jnp.bfloat16)
        side_parts = jnp.stack([key_part, value_part]).reshape(pair_rim.shape)
        return (query_part.astype(jnp.bfloat16).reshape(query_head.shape), side_parts)

    query_grad, side_parts = lax.map(head_returned, (queries, out_grad, pair_rims))
    upper_band = side_parts[:, :, :, 0:tile_size]
    middle_rows = side_parts[:, :, :, tile_size : 2 * tile_size]
    lower_band = side_parts[:, :, :, 2 * tile_size : 3 * tile_size]
    below_parts = passed_along(upper_band, "sy", -1)
    above_parts = passed_along(lower_band, "sy", 1)
    row_sum = (
        middle_rows.astype(jnp.float32)
        + below_parts.astype(jnp.float32)
        + above_parts.astype(jnp.float32)
    )
    left_tile = row_sum[:, :, :, :, 0:tile_size]
    centre_tile = row_sum[:, :, :, :, tile_size : 2 * tile_size]
    right_tile = row_sum[:, :, :, :, 2 * tile_size : 3 * tile_size]
    right_parts = passed_along(left_tile, "sx", -1)
    left_parts = passed_along(right_tile, "sx", 1)
    side_total = centre_tile + right_parts + left_parts
    key_grad = side_total[:, 0].astype(jnp.bfloat16)
    value_grad = side_total[:, 1].astype(jnp.bfloat16)
    return (query_grad, key_grad, value_grad)


def solution(mesh):
    return jax.shard_map(
        local,
        mesh=mesh,
        in_specs=(
            P("tp", None, "sy", "sx", None),
            P("tp", None, "sy", "sx", None),
            P("tp", None, "sy", "sx", None),
            P("tp", None, "sy", "sx", None),
            P(),
        ),
        out_specs=(
            P("tp", None, "sy", "sx", None),
            P("tp", None, "sy", "sx", None),
            P("tp", None, "sy", "sx", None),
        ),
        check_vma=False,
    )
```

profile of v0, /device:TPU:26, one launch (start us, length us, event | category | flops | bytes accessed | tf_op | source)
XLA Modules:
  0.0 554.7 jit_solution(11120715627684831092)
XLA Ops:
  0.6 1.2 pad_maximum_fusion.2
  1.9 2.1 collective-permute-start.1
  3.9 2.4 collective-permute-start
  6.3 7.1 %collective-permute-done.1 = bf16[6,2,4,8,8,128]{5,4,3,2,1,0:T(8,128)(2,1)S(1)} collective-permute-done((bf16[6,2,4,8,8,128]{5,4,3,2,1,0:T(8,128)(2,1)S(1)}, bf16[6,2,4,8,8,128]{5,4,3,2,1,0:T(8,128)(2,1)S(1)}, u32[]{:S(2)}, u32[]{:S(2)}) %collective-permute-start.1) | collective-permute-done | bytes 786464 | tf_op jit(solution)/shard_map/ppermute | solution.py:17
  13.4 3.8 collective-permute-done
  17.2 2.8 pad_maximum_fusion.1
  20.0 9.3 %collective-permute-start.3 = (bf16[6,2,4,24,8,128]{5,4,3,2,1,0:T(8,128)(2,1)}, bf16[6,2,4,24,8,128]{5,4,3,2,1,0:T(8,128)(2,1)}, u32[]{:S(2)}, u32[]{:S(2)}) collective-permute-start(bf16[6,2,4,24,8,128]{5,4,3,2,1,0:T(8,128)(2,1)} %pad_maximum_fusion.1), channel_id=1, source_target_pairs={{1,0},{2,1},{3,2},{4,3},{5,4},{6,5},{7,6},{9,8},{10,9},{11,10},{12... | collective-permute-start | bytes 7077896 | tf_op jit(solution)/shard_map/ppermute | solution.py:17
  29.3 2.5 collective-permute-start.2
  32.3 99.9 %collective-permute-done.3 = bf16[6,2,4,24,8,128]{5,4,3,2,1,0:T(8,128)(2,1)} collective-permute-done((bf16[6,2,4,24,8,128]{5,4,3,2,1,0:T(8,128)(2,1)}, bf16[6,2,4,24,8,128]{5,4,3,2,1,0:T(8,128)(2,1)}, u32[]{:S(2)}, u32[]{:S(2)}) %collective-permute-start.3) | collective-permute-done | bytes 2359328 | tf_op jit(solution)/shard_map/ppermute | solution.py:17
  132.2 80.8 %collective-permute-done.2 = bf16[6,2,4,24,8,128]{5,4,3,2,1,0:T(8,128)(2,1)} collective-permute-done((bf16[6,2,4,24,8,128]{5,4,3,2,1,0:T(8,128)(2,1)}, bf16[6,2,4,24,8,128]{5,4,3,2,1,0:T(8,128)(2,1)}, u32[]{:S(2)}, u32[]{:S(2)}) %collective-permute-start.2) | collective-permute-done | bytes 2359328 | tf_op jit(solution)/shard_map/ppermute | solution.py:14
  213.0 6.1 %pad_maximum_fusion = bf16[6,2,4,24,24,128]{5,4,3,2,1,0:T(8,128)(2,1)} fusion(bf16[6,2,4,24,8,128]{5,4,3,2,1,0:T(8,128)(2,1)} %collective-permute-done.3, bf16[6,2,4,8,8,128]{5,4,3,2,1,0:T(8,128)(2,1)S(1)} %collective-permute-done.1, bf16[6,1,4,8,8,128]{5,4,3,2,1,0:T(8,128)(2,1)S(1)} %bitcast.79, bf16[6,1,4,8,8,128]{5,4,3,2,1,0:T(8,128)(2,1)S(1)} %bitcast.82, ...), kind=kLoop, calls=%fused_computation.28 | loop fusion | flops 42467328 | bytes 14155776 | tf_op jit(solution)/shard_map/concatenate | solution.py:18
  219.1 132.3 %while.13 = (s32[]{:T(128)}, bf16[6,4,8,8,128]{4,3,2,1,0:T(8,128)(2,1)}, bf16[6,2,4,24,24,128]{5,4,3,2,0,1:T(8,128)(2,1)}, bf16[6,4,8,8,128]{4,3,2,1,0:T(8,128)(...) while((s32[]{:T(128)}, ...), condition=%wide.region_4.5_spmd.clone, body=%wide.region_0.4_spmd.clone.sunk | while | flops 917635072 | bytes 39895592 | solution.py:108
  219.2 0.9 constant_dynamic-slice_fusion.6
  220.2 2.5 constant_dynamic-slice_fusion.7
  222.6 1.0 broadcast_in_dim.87
  223.6 8.7 %reshape.113 = pred[256,2304]{1,0:T(32,128)(4,1)} reshape(pred[4,8,8,4,24,24]{5,4,3,2,1,0:T(8,128)(4,1)S(1)} %broadcast_in_dim.87) | data formatting | bytes 1179648 | tf_op jit(solution)/shard_map/reshape | solution.py:43
  232.4 2.0 select_reduce_fusion.2
  235.0 0.8 fusion.61
  239.9 1.2 fusion.66
  241.2 0.9 constant_dynamic-slice_fusion.6
  242.2 2.5 constant_dynamic-slice_fusion.7
  244.6 1.0 broadcast_in_dim.87
  245.7 8.7 %reshape.113 = pred[256,2304]{1,0:T(32,128)(4,1)} reshape(pred[4,8,8,4,24,24]{5,4,3,2,1,0:T(8,128)(4,1)S(1)} %broadcast_in_dim.87) | data formatting | bytes 1179648 | tf_op jit(solution)/shard_map/reshape | solution.py:43
  254.4 2.0 select_reduce_fusion.2
  257.1 0.8 fusion.61
  261.9 1.2 fusion.66
  263.2 0.9 constant_dynamic-slice_fusion.6
  264.2 2.5 constant_dynamic-slice_fusion.7
  266.7 1.0 broadcast_in_dim.87
  267.7 8.7 %reshape.113 = pred[256,2304]{1,0:T(32,128)(4,1)} reshape(pred[4,8,8,4,24,24]{5,4,3,2,1,0:T(8,128)(4,1)S(1)} %broadcast_in_dim.87) | data formatting | bytes 1179648 | tf_op jit(solution)/shard_map/reshape | solution.py:43
  276.4 2.0 select_reduce_fusion.2
  279.1 0.8 fusion.61
  283.9 1.3 fusion.66
  285.3 0.9 constant_dynamic-slice_fusion.6
  286.3 2.5 constant_dynamic-slice_fusion.7
  288.8 1.0 broadcast_in_dim.87
  289.8 8.7 %reshape.113 = pred[256,2304]{1,0:T(32,128)(4,1)} reshape(pred[4,8,8,4,24,24]{5,4,3,2,1,0:T(8,128)(4,1)S(1)} %broadcast_in_dim.87) | data formatting | bytes 1179648 | tf_op jit(solution)/shard_map/reshape | solution.py:43
  298.5 2.0 select_reduce_fusion.2
  301.2 0.8 fusion.61
  306.0 1.3 fusion.66
  307.4 0.9 constant_dynamic-slice_fusion.6
  308.4 2.5 constant_dynamic-slice_fusion.7
  310.9 1.0 broadcast_in_dim.87
  311.9 8.7 %reshape.113 = pred[256,2304]{1,0:T(32,128)(4,1)} reshape(pred[4,8,8,4,24,24]{5,4,3,2,1,0:T(8,128)(4,1)S(1)} %broadcast_in_dim.87) | data formatting | bytes 1179648 | tf_op jit(solution)/shard_map/reshape | solution.py:43
  320.6 2.0 select_reduce_fusion.2
  323.3 0.8 fusion.61
  328.1 1.3 fusion.66
  329.5 0.9 constant_dynamic-slice_fusion.6
  330.5 2.5 constant_dynamic-slice_fusion.7
  333.0 1.0 broadcast_in_dim.87
  334.0 8.7 %reshape.113 = pred[256,2304]{1,0:T(32,128)(4,1)} reshape(pred[4,8,8,4,24,24]{5,4,3,2,1,0:T(8,128)(4,1)S(1)} %broadcast_in_dim.87) | data formatting | bytes 1179648 | tf_op jit(solution)/shard_map/reshape | solution.py:43
  342.7 2.0 select_reduce_fusion.2
  350.2 1.2 fusion.66
  351.4 3.2 fusion.17
  354.6 1.9 collective-permute-start.4
  356.6 2.4 collective-permute-start.5
  359.0 23.9 %collective-permute-done.4 = bf16[6,2,4,8,24,128]{5,4,3,2,0,1:T(8,128)(2,1)S(1)} collective-permute-done((bf16[6,2,4,8,24,128]{5,4,3,2,0,1:T(8,128)(2,1)S(1)}, bf16[6,2,4,8,24,128]{5,4,3,2,0,1:T(8,128)(2,1)S(1)}, u32[]{:S(2)}, u32[]{:S(2)}) %collective-permute-start.4) | collective-permute-done | bytes 2359328 | tf_op jit(solution)/shard_map/ppermute | solution.py:25
  382.9 3.8 collective-permute-done.5
  386.7 2.8 convert_add_fusion
  390.0 27.6 %collective-permute-start.6 = (f32[6,2,4,8,8,128]{5,4,3,2,0,1:T(8,128)S(1)}, f32[6,2,4,8,8,128]{5,4,3,2,0,1:T(8,128)S(1)}, u32[]{:S(2)}, u32[]{:S(2)}) collective-permute-start(f32[6,2,4,8,8,128]{5,4,3,2,0,1:T(8,128)S(1)} %get-tuple-element.101), channel_id=1, source_target_pairs={{1,0},{2,1},{3,2},{4,3},{5,4},{6,5},{7,6},{9,8},{10,9},{11,10},{12... | collective-permute-start | bytes 4718600 | tf_op jit(solution)/shard_map/ppermute | solution.py:25
  417.6 1.9 collective-permute-start.7
  419.5 66.8 %collective-permute-done.6 = f32[6,2,4,8,8,128]{5,4,3,2,0,1:T(8,128)S(1)} collective-permute-done((f32[6,2,4,8,8,128]{5,4,3,2,0,1:T(8,128)S(1)}, f32[6,2,4,8,8,128]{5,4,3,2,0,1:T(8,128)S(1)}, u32[]{:S(2)}, u32[]{:S(2)}) %collective-permute-start.6) | collective-permute-done | bytes 1572896 | tf_op jit(solution)/shard_map/ppermute | solution.py:25
  486.3 67.0 %collective-permute-done.7 = f32[6,2,4,8,8,128]{5,4,3,2,0,1:T(8,128)S(1)} collective-permute-done((f32[6,2,4,8,8,128]{5,4,3,2,0,1:T(8,128)S(1)}, f32[6,2,4,8,8,128]{5,4,3,2,0,1:T(8,128)S(1)}, u32[]{:S(2)}, u32[]{:S(2)}) %collective-permute-start.7) | collective-permute-done | bytes 1572896 | tf_op jit(solution)/shard_map/ppermute | solution.py:25
  553.8 0.9 slice_bitcast_fusion
  (124 shorter events, 31.3 us)
Async XLA Ops:
  1.8 30.0 %copy-start.5 = (s32[64,64]{1,0:T(8,128)S(1)}, s32[64,64]{1,0:T(8,128)}, u32[]{:S(2)}) copy-start(s32[64,64]{1,0:T(8,128)} %param.11) | copy-start | bytes 49156
  1.8 211.2 %copy-start.3 = (bf16[6,4,8,8,128]{4,3,2,1,0:T(8,128)(2,1)S(1)}, bf16[6,4,8,8,128]{4,3,2,1,0:T(8,128)(2,1)}, u32[]{:S(2)}) copy-start(bf16[6,4,8,8,128]{4,3,2,1,0:T(8,128)(2,1)} %param.9) | copy-start | bytes 1179652
  1.9 211.1 %copy-start.4 = (bf16[6,4,8,8,128]{4,3,2,1,0:T(8,128)(2,1)S(1)}, bf16[6,4,8,8,128]{4,3,2,1,0:T(8,128)(2,1)}, u32[]{:S(2)}) copy-start(bf16[6,4,8,8,128]{4,3,2,1,0:T(8,128)(2,1)} %param.8) | copy-start | bytes 1179652
  1.9 11.5 %collective-permute-start.1 = (bf16[6,2,4,8,8,128]{5,4,3,2,1,0:T(8,128)(2,1)S(1)}, bf16[6,2,4,8,8,128]{5,4,3,2,1,0:T(8,128)(2,1)S(1)}, u32[]{:S(2)}, u32[]{:S(2)}) collective-permute-start(bf16[6,2,4,8,8,128]{5,4,3,2,1,0:T(8,128)(2,1)S(1)} %pad_maximum_fusion.2), channel_id=1, source_target_pairs={{8,0},{16,8},{24,16},{32,24},{40,32},{48,40},{56,48},{9,1},{17,9},... | collective-permute-start | bytes 2359304 | tf_op jit(solution)/shard_map/ppermute | solution.py:17
  3.9 13.3 %collective-permute-start = (bf16[6,2,4,8,8,128]{5,4,3,2,1,0:T(8,128)(2,1)S(1)}, bf16[6,2,4,8,8,128]{5,4,3,2,1,0:T(8,128)(2,1)S(1)}, u32[]{:S(2)}, u32[]{:S(2)}) collective-permute-start(bf16[6,2,4,8,8,128]{5,4,3,2,1,0:T(8,128)(2,1)S(1)} %pad_maximum_fusion.2), channel_id=1, source_target_pairs={{0,8},{8,16},{16,24},{24,32},{32,40},{40,48},{48,56},{1,9},{9,17},... | collective-permute-start | bytes 2359304 | tf_op jit(solution)/shard_map/ppermute | solution.py:14
  20.0 112.2 %collective-permute-start.3 = (bf16[6,2,4,24,8,128]{5,4,3,2,1,0:T(8,128)(2,1)}, bf16[6,2,4,24,8,128]{5,4,3,2,1,0:T(8,128)(2,1)}, u32[]{:S(2)}, u32[]{:S(2)}) collective-permute-start(bf16[6,2,4,24,8,128]{5,4,3,2,1,0:T(8,128)(2,1)} %pad_maximum_fusion.1), channel_id=1, source_target_pairs={{1,0},{2,1},{3,2},{4,3},{5,4},{6,5},{7,6},{9,8},{10,9},{11,10},{12... | collective-permute-start | bytes 7077896 | tf_op jit(solution)/shard_map/ppermute | solution.py:17
  29.3 183.7 %collective-permute-start.2 = (bf16[6,2,4,24,8,128]{5,4,3,2,1,0:T(8,128)(2,1)}, bf16[6,2,4,24,8,128]{5,4,3,2,1,0:T(8,128)(2,1)}, u32[]{:S(2)}, u32[]{:S(2)}) collective-permute-start(bf16[6,2,4,24,8,128]{5,4,3,2,1,0:T(8,128)(2,1)} %pad_maximum_fusion.1), channel_id=1, source_target_pairs={{0,1},{1,2},{2,3},{3,4},{4,5},{5,6},{6,7},{8,9},{9,10},{10,11},{11... | collective-permute-start | bytes 7077896 | tf_op jit(solution)/shard_map/ppermute | solution.py:14
  232.3 2.0 copy-start
  235.0 1.1 copy-start.1
  237.2 1.1 copy-start.2
  254.4 2.0 copy-start
  257.0 1.1 copy-start.1
  259.2 1.1 copy-start.2
  276.4 2.0 copy-start
  279.1 1.1 copy-start.1
  281.2 1.1 copy-start.2
  298.5 2.0 copy-start
  301.2 1.1 copy-start.1
  303.3 1.1 copy-start.2
  320.6 2.0 copy-start
  323.3 1.1 copy-start.1
  325.4 1.1 copy-start.2
  342.7 2.0 copy-start
  345.4 1.1 copy-start.1
  347.5 1.1 copy-start.2
  354.6 28.3 %collective-permute-start.4 = (bf16[6,2,4,8,24,128]{5,4,3,2,0,1:T(8,128)(2,1)S(1)}, bf16[6,2,4,8,24,128]{5,4,3,2,0,1:T(8,128)(2,1)S(1)}, u32[]{:S(2)}, u32[]{:S(2)}) collective-permute-start(bf16[6,2,4,8,24,128]{5,4,3,2,0,1:T(8,128)(2,1)S(1)} %get-tuple-element.99), channel_id=1, source_target_pairs={{8,0},{16,8},{24,16},{32,24},{40,32},{48,40},{56,48},{9,1},{17,9},... | collective-permute-start | bytes 7077896 | tf_op jit(solution)/shard_map/ppermute | solution.py:25
  356.6 30.2 %collective-permute-start.5 = (bf16[6,2,4,8,24,128]{5,4,3,2,0,1:T(8,128)(2,1)S(1)}, bf16[6,2,4,8,24,128]{5,4,3,2,0,1:T(8,128)(2,1)S(1)}, u32[]{:S(2)}, u32[]{:S(2)}) collective-permute-start(bf16[6,2,4,8,24,128]{5,4,3,2,0,1:T(8,128)(2,1)S(1)} %get-tuple-element.100), channel_id=1, source_target_pairs={{0,8},{8,16},{16,24},{24,32},{32,40},{40,48},{48,56},{1,9},{9,17},... | collective-permute-start | bytes 7077896 | tf_op jit(solution)/shard_map/ppermute | solution.py:25
  390.0 96.3 %collective-permute-start.6 = (f32[6,2,4,8,8,128]{5,4,3,2,0,1:T(8,128)S(1)}, f32[6,2,4,8,8,128]{5,4,3,2,0,1:T(8,128)S(1)}, u32[]{:S(2)}, u32[]{:S(2)}) collective-permute-start(f32[6,2,4,8,8,128]{5,4,3,2,0,1:T(8,128)S(1)} %get-tuple-element.101), channel_id=1, source_target_pairs={{1,0},{2,1},{3,2},{4,3},{5,4},{6,5},{7,6},{9,8},{10,9},{11,10},{12... | collective-permute-start | bytes 4718600 | tf_op jit(solution)/shard_map/ppermute | solution.py:25
  417.6 135.8 %collective-permute-start.7 = (f32[6,2,4,8,8,128]{5,4,3,2,0,1:T(8,128)S(1)}, f32[6,2,4,8,8,128]{5,4,3,2,0,1:T(8,128)S(1)}, u32[]{:S(2)}, u32[]{:S(2)}) collective-permute-start(f32[6,2,4,8,8,128]{5,4,3,2,0,1:T(8,128)S(1)} %get-tuple-element.102), channel_id=1, source_target_pairs={{0,1},{1,2},{2,3},{3,4},{4,5},{5,6},{6,7},{8,9},{9,10},{10,11},{11... | collective-permute-start | bytes 4718600 | tf_op jit(solution)/shard_map/ppermute | solution.py:25
where the time goes:
time: 556 us; the launch traced here: 555 us
  waiting for transfers between devices  353 us (63%)
  local copies, waits for them, and re-layouts  92.8 us (17%)
  starting transfers between devices  50.1 us (9%)
  other arithmetic  30.2 us (5%)
  matrix products  27.1 us (5%)
    ppermute x4, waiting for transfers between devices, passed_along(): return lax.ppermute(block, axis, route)  162 us
    ppermute x2, waiting for transfers between devices, extended(): lax.ppermute(lax.slice_in_dim(block, 0, width, axis=dim), axis, backward)  107 us
    ppermute x2, waiting for transfers between devices, extended(): lax.ppermute(lax.slice_in_dim(block, block.shape[dim] - width, None, axis...  84.6 us
    reshape x6, local copies, waits for them, and re-layouts, window_mask(): allowed.reshape(frames * tile_size * tile_size, frames * rim_span * rim_s...  52.2 us
    ppermute x4, starting transfers between devices, passed_along(): return lax.ppermute(block, axis, route)  33.8 us
    slice x6, local copies, waits for them, and re-layouts, head_returned(): pair_rim[1].reshape(-1, width)  14.8 us
    dot_general x12, matrix products, contract_last(): lax.dot_general(left_rows, right_rows, (((1,), (1,)), ((), ())), preferre...  14.7 us
    ppermute x2, starting transfers between devices, extended(): lax.ppermute(lax.slice_in_dim(block, 0, width, axis=dim), axis, backward)  11.3 us
  transfers between devices with their start and end apart: 8, of which 8 were waited for; matrix products, arithmetic and copies ran while one was open for 0% of the time, Pallas kernels for 0%

commit v1 on v0

v1 whole, which is shorter than its diff:
```python
import functools
import math

import jax
import jax.numpy as jnp
from jax import lax
from jax.experimental import pallas as pl
from jax.experimental.pallas import tpu as pltpu
from jax.sharding import PartitionSpec as P

MESH = pl.DeviceIdType.MESH
NEG = -1e30


def rows_by_rows(left, right):
    return lax.dot_general(
        left, right, (((1,), (1,)), ((), ())), preferred_element_type=jnp.float32
    )


def columns_by_columns(left, right):
    return lax.dot_general(
        left, right, (((0,), (0,)), ((), ())), preferred_element_type=jnp.float32
    )


def fold_rows(x, op):
    x = x.reshape(x.shape[0] // 8, 8, x.shape[1])
    return op(x, axis=0)


def kernel(
    sizes,
    q_hbm,
    k_hbm,
    v_hbm,
    g_hbm,
    valid_hbm,
    dq_hbm,
    dk_hbm,
    dv_hbm,
    kv,
    qg,
    part,
    from_rows,
    y_out,
    y_in,
    z_out,
    bias,
    s_buf,
    dp_buf,
    p_low,
    ds_low,
    scaled,
    by_lane,
    valid_ref,
    valid_sem,
    zin_send,
    zin_recv,
    yk_send,
    yk_recv,
    rk_send,
    rk_recv,
    rg_send,
    rg_recv,
    yg_send,
    yg_recv,
    zo_send,
    zo_recv,
):
    n_tp, n_sy, n_sx, heads, tile, frames, tokens, width = sizes
    n_y = n_sx // 2
    ring = 2 * n_tp
    hop = n_tp // 2
    half = heads // 2
    cells = tile * tile
    scale = 1.0 / math.sqrt(width)
    alpha = scale * math.log2(math.e)

    tp = lax.axis_index("tp")
    sy = lax.axis_index("sy")
    sx = lax.axis_index("sx")
    y = sx // 2
    zh = lax.rem(sx, 2)
    z = zh * n_tp + tp

    def z_peer(step):
        other = lax.rem(z + step + ring, ring)
        return other // n_tp, (lax.rem(other, n_tp), sy, y * 2 + other // n_tp)

    def y_peer(step):
        return (tp, sy, lax.rem(y + step + n_y, n_y) * 2 + zh)

    def row_peer(step):
        return (tp, lax.rem(sy + step + n_sy, n_sy), sx)

    up_side, up = z_peer(hop)
    down_side, down = z_peer(-hop)
    z_peers = (up, down)
    z_sides = (up_side, down_side)
    y_peers = (y_peer(-1), y_peer(1))
    row_peers = (row_peer(-1), row_peer(1))

    def copy(src, dst, send, recv, where):
        return pltpu.make_async_remote_copy(
            src_ref=src,
            dst_ref=dst,
            send_sem=send,
            recv_sem=recv,
            device_id=where,
            device_id_type=MESH,
        )

    barrier = pltpu.get_barrier_semaphore()
    for where in (*z_peers, *y_peers, *row_peers):
        pl.semaphore_signal(barrier, inc=1, device_id=where, device_id_type=MESH)
    fetch = pltpu.make_async_copy(valid_hbm, valid_ref, valid_sem)
    fetch.start()
    pl.semaphore_wait(barrier, 6)

    sources = (k_hbm, v_hbm, q_hbm, g_hbm)

    def zin_slot(t, h, side):
        if t < 2:
            return kv.at[t, h, 1, 1 + side]
        return qg.at[t - 2, h, side]

    def zin(t, h, way):
        which = zh if way == 0 else 1 - zh
        return copy(
            sources[t].at[which * half + h],
            zin_slot(t, h, zh),
            zin_send.at[t, h, way],
            zin_recv.at[t, h, zh],
            z_peers[way],
        )

    def zin_arrival(t, h, side):
        slot = zin_slot(t, h, side)
        return copy(slot, slot, zin_send.at[t, h, 0], zin_recv.at[t, h, side], up)

    def y_halo(t, h, way):
        src = kv.at[t, h, 1, 1 if way == 0 else 2]
        dst = kv.at[t, h, 1, 3 if way == 0 else 0]
        return copy(src, dst, yk_send.at[t, h, way], yk_recv.at[t, h, way], y_peers[way])

    def row_halo(t, h, way):
        return copy(
            kv.at[t, h, 1],
            kv.at[t, h, 2 if way == 0 else 0],
            rk_send.at[t, h, way],
            rk_recv.at[t, h, way],
            row_peers[way],
        )

    def row_grad(t, h, way):
        return copy(
            part.at[t, h, way],
            from_rows.at[t, h, way],
            rg_send.at[t, h, way],
            rg_recv.at[t, h, way],
            row_peers[way],
        )

    def y_grad(t, h, way):
        return copy(
            y_out.at[t, h, way],
            y_in.at[t, h, way],
            yg_send.at[t, h, way],
            yg_recv.at[t, h, way],
            y_peers[way],
        )

    in_first = jnp.logical_and(z >= hop, z < ring - hop)
    first_head = jnp.where(in_first, 0, half)
    results = (dk_hbm, dv_hbm, dq_hbm)

    def zout(t, h, way):
        return copy(
            z_out.at[t, h, z_sides[way]],
            results[t].at[first_head + h],
            zo_send.at[t, h, way],
            zo_recv.at[t, first_head + h],
            z_peers[way],
        )

    def start_in(tensors, h):
        for t in tensors:
            for way in (0, 1):
                zin(t, h, way).start()

    start_in((0, 1), 0)
    start_in((2, 3), 0)

    fetch.wait()
    valid = valid_ref[...].astype(jnp.float32).astype(jnp.bfloat16)
    grid_rows, grid_columns = valid.shape
    lane = lax.broadcasted_iota(jnp.int32, (cells, tokens), 1)
    cell = lax.broadcasted_iota(jnp.int32, (cells, tokens), 0)
    bits = tile.bit_length() - 1
    k_row, k_col = cell >> bits, cell & (tile - 1)
    q_row, q_col = (lane >> bits) & (tile - 1), lane & (tile - 1)
    sel_lane_r = lax.broadcasted_iota(jnp.int32, (cells, grid_rows), 1)
    sel_cell_r = lax.broadcasted_iota(jnp.int32, (cells, grid_rows), 0)
    sel_lane_c = lax.broadcasted_iota(jnp.int32, (cells, grid_columns), 1)
    sel_cell_c = lax.broadcasted_iota(jnp.int32, (cells, grid_columns), 0)
    ones = jnp.ones((grid_columns, tokens), jnp.bfloat16)

    def as_low(mask):
        return jnp.where(mask, 1.0, 0.0).astype(jnp.bfloat16)

    q_live = []
    for ct in range(2):
        col_lane = lax.broadcasted_iota(jnp.int32, (grid_columns, tokens), 1)
        col_cell = lax.broadcasted_iota(jnp.int32, (grid_columns, tokens), 0)
        pick = as_low(col_cell == (2 * y + ct) * tile + (col_lane & (tile - 1)))
        by_row = jnp.dot(valid, pick, preferred_element_type=jnp.float32)
        row_lane = lax.broadcasted_iota(jnp.int32, (grid_rows, tokens), 1)
        row_cell = lax.broadcasted_iota(jnp.int32, (grid_rows, tokens), 0)
        mine = row_cell == sy * tile + ((row_lane >> bits) & (tile - 1))
        q_live.append(jnp.sum(jnp.where(mine, by_row, 0.0), axis=0, keepdims=True))

    for r in range(3):
        pick_row = as_low(sel_lane_r == (sy - 1 + r) * tile + (sel_cell_r >> bits))
        by_cell = jnp.dot(pick_row, valid, preferred_element_type=jnp.float32)
        row_ok = jnp.abs((r - 1) * tile + k_row - q_row) <= tile
        for c in range(4):
            at_col = sel_lane_c == (2 * y - 1 + c) * tile + (sel_cell_c & (tile - 1))
            one = jnp.where(at_col, by_cell, 0.0).astype(jnp.bfloat16)
            k_live = jnp.dot(one, ones, preferred_element_type=jnp.float32)
            for ct in range(2):
                if 0 <= c - ct <= 2:
                    col_ok = jnp.abs((c - ct - 1) * tile + k_col - q_col) <= tile
                    ok = jnp.where(row_ok & col_ok, k_live * q_live[ct], 0.0)
                    bias[ct, r, c - ct] = jnp.where(ok > 0.5, 0.0, NEG)

    def relay_columns(h):
        for t in (0, 1):
            for way in (0, 1):
                zin_arrival(t, h, way).wait_recv()
                y_halo(t, h, way).start()

    def relay_rows(h):
        for t in (0, 1):
            for way in (0, 1):
                y_halo(t, h, way).wait_recv()
            for way in (0, 1):
                row_halo(t, h, way).start()

    def attend(h, ct):
        q = qg[0, h, ct]
        g = qg[1, h, ct]
        lanes = pl.ds(pl.multiple_of(ct * tokens, tokens), tokens)
        top = jnp.full((8, tokens), NEG, jnp.float32)
        for r in range(3):
            for c in range(3):
                s = rows_by_rows(kv[0, h, r, ct + c], q) * alpha
                s = s.reshape(frames, cells, tokens) + bias[ct, r, c][None]
                s = s.reshape(tokens, tokens)
                s_buf[r, c] = s
                top = jnp.maximum(top, fold_rows(s, jnp.max))
        top = jnp.max(top, axis=0, keepdims=True)

        total = jnp.zeros((8, tokens), jnp.float32)
        delta = jnp.zeros((8, tokens), jnp.float32)
        for r in range(3):
            for c in range(3):
                p = jnp.exp2(s_buf[r, c] - top)
                dp = rows_by_rows(kv[1, h, r, ct + c], g)
                s_buf[r, c] = p
                dp_buf[r, c] = dp
                p_low[r, ct + c, :, lanes] = p.astype(jnp.bfloat16)
                total = total + fold_rows(p, jnp.sum)
                delta = delta + fold_rows(p * dp, jnp.sum)
        total = jnp.sum(total, axis=0, keepdims=True)
        inverse = jnp.where(top > 0.1 * NEG, 1.0 / total, 0.0)
        delta = jnp.sum(delta, axis=0, keepdims=True) * inverse

        for r in range(3):
            for c in range(3):
                ds = s_buf[r, c] * (dp_buf[r, c] - delta)
                ds_low[r, ct + c, :, lanes] = ds.astype(jnp.bfloat16)

        inverse = jnp.broadcast_to(inverse, (width, tokens))
        by_token = inverse.T
        rows = lanes
        scaled[0, rows] = (q.astype(jnp.float32) * (by_token * scale)).astype(jnp.bfloat16)
        scaled[1, rows] = (g.astype(jnp.float32) * by_token).astype(jnp.bfloat16)
        by_lane[ct] = inverse * scale

    def key_products(h, r):
        where = {0: 0, 2: 1, 1: 2}[r]
        for t, low in ((0, ds_low), (1, p_low)):
            for c in range(4):
                first, last = max(c - 2, 0), min(c, 1)
                lanes = slice(first * tokens, (last + 1) * tokens)
                part[t, h, where, c] = jnp.dot(
                    low[r, c, :, lanes], scaled[t, lanes], preferred_element_type=jnp.float32
                ).astype(jnp.bfloat16)

    def query_products(h):
        for ct in range(2):
            lanes = slice(ct * tokens, (ct + 1) * tokens)
            dq = jnp.zeros((width, tokens), jnp.float32)
            for r in range(3):
                keys = kv[0, h, r, ct : ct + 3].reshape(3 * tokens, width)
                ds = ds_low[r, ct : ct + 3, :, lanes].reshape(3 * tokens, tokens)
                dq = dq + columns_by_columns(keys, ds)
            z_out[2, h, ct] = (dq * by_lane[ct]).T.astype(jnp.bfloat16)

    def add_rows(h):
        for t in (0, 1):
            for way in (0, 1):
                row_grad(t, h, way).wait_recv()
            for way, c in ((0, 0), (1, 3)):
                y_out[t, h, way] = (
                    part[t, h, 2, c].astype(jnp.float32)
                    + from_rows[t, h, 0, c].astype(jnp.float32)
                    + from_rows[t, h, 1, c].astype(jnp.float32)
                ).astype(jnp.bfloat16)
            for way in (0, 1):
                y_grad(t, h, way).start()

    def add_columns(h):
        for t in (0, 1):
            for way in (0, 1):
                y_grad(t, h, way).wait_recv()
            for side in (0, 1):
                z_out[t, h, side] = (
                    part[t, h, 2, 1 + side].astype(jnp.float32)
                    + from_rows[t, h, 0, 1 + side].astype(jnp.float32)
                    + from_rows[t, h, 1, 1 + side].astype(jnp.float32)
                    + y_in[t, h, 1 - side].astype(jnp.float32)
                ).astype(jnp.bfloat16)
            for way in (0, 1):
                zout(t, h, way).start()

    def wait_queries(h):
        for t in (2, 3):
            for way in (0, 1):
                zin_arrival(t, h, way).wait_recv()

    def wait_rows(h):
        for t in (0, 1):
            for way in (0, 1):
                row_halo(t, h, way).wait_recv()

    def attend_both(h):
        def step(ct, unused):
            attend(h, ct)
            return unused

        lax.fori_loop(0, 2, step, 0)

    def products(h):
        for way, r in ((0, 0), (1, 2)):
            key_products(h, r)
            for t in (0, 1):
                row_grad(t, h, way).start()
        key_products(h, 1)
        query_products(h)

    def send_queries(h):
        for way in (0, 1):
            zout(2, h, way).start()

    last = half - 1
    relay_columns(0)
    start_in((0, 1), 1)
    relay_rows(0)
    wait_queries(0)
    start_in((0, 1), 2)
    for h in range(half):
        wait_rows(h)
        if h >= 1:
            wait_queries(h)
        attend_both(h)
        if h == 0:
            relay_columns(1)
            start_in((2, 3), 1)
        if h == 1:
            add_columns(0)
        if h == 2:
            add_rows(1)
        products(h)
        if h == 0:
            relay_rows(1)
            relay_columns(2)
            start_in((2, 3), 2)
            send_queries(0)
            add_rows(0)
            relay_rows(2)
        else:
            send_queries(h)
    add_columns(last - 1)
    add_rows(last)
    for h in range(half):
        for way in (0, 1):
            for t in range(4):
                zin(t, h, way).wait_send()
            for t in range(2):
                y_halo(t, h, way).wait_send()
                row_halo(t, h, way).wait_send()
                row_grad(t, h, way).wait_send()
    add_columns(last)
    for h in range(half):
        for way in (0, 1):
            for t in range(2):
                y_grad(t, h, way).wait_send()
            for t in range(3):
                zout(t, h, way).wait_send()
    for t in range(3):
        for h in range(heads):
            slot = results[t].at[h]
            copy(slot, slot, zo_send.at[t, 0, 0], zo_recv.at[t, h], up).wait_recv()


def local(mesh_sizes, queries, key_vectors, value_vectors, out_grad, cell_valid):
    n_tp, n_sy, n_sx = mesh_sizes
    heads, frames, tile, _, width = queries.shape
    tokens = frames * tile * tile
    half = heads // 2
    cells = tile * tile
    sizes = (n_tp, n_sy, n_sx, heads, tile, frames, tokens, width)
    flat = [
        x.reshape(heads, tokens, width) for x in (queries, key_vectors, value_vectors, out_grad)
    ]
    low = jnp.bfloat16
    dma = pltpu.SemaphoreType.DMA
    out = pltpu.VMEM((heads, tokens, width), low)
    anywhere = pl.BlockSpec(memory_space=pl.ANY)
    results = pl.pallas_call(
        functools.partial(kernel, sizes),
        name="window_backward",
        out_shape=(out, out, out),
        in_specs=[pl.BlockSpec(memory_space=pltpu.HBM)] * 5,
        out_specs=(anywhere, anywhere, anywhere),
        scratch_shapes=[
            pltpu.VMEM((2, half, 3, 4, tokens, width), low),
            pltpu.VMEM((2, half, 2, tokens, width), low),
            pltpu.VMEM((2, half, 3, 4, tokens, width), low),
            pltpu.VMEM((2, half, 2, 4, tokens, width), low),
            pltpu.VMEM((2, half, 2, tokens, width), low),
            pltpu.VMEM((2, half, 2, tokens, width), low),
            pltpu.VMEM((3, half, 2, tokens, width), low),
            pltpu.VMEM((2, 3, 3, cells, tokens), jnp.float32),
            pltpu.VMEM((3, 3, tokens, tokens), jnp.float32),
            pltpu.VMEM((3, 3, tokens, tokens), jnp.float32),
            pltpu.VMEM((3, 4, tokens, 2 * tokens), low),
            pltpu.VMEM((3, 4, tokens, 2 * tokens), low),
            pltpu.VMEM((2, 2 * tokens, width), low),
            pltpu.VMEM((2, width, tokens), jnp.float32),
            pltpu.VMEM(cell_valid.shape, cell_valid.dtype),
            dma(()),
            dma((4, half, 2)),
            dma((4, half, 2)),
            dma((2, half, 2)),
            dma((2, half, 2)),
            dma((2, half, 2)),
            dma((2, half, 2)),
            dma((2, half, 2)),
            dma((2, half, 2)),
            dma((2, half, 2)),
            dma((2, half, 2)),
            dma((3, half, 2)),
            dma((3, heads)),
        ],
        compiler_params=pltpu.CompilerParams(
            collective_id=0, has_side_effects=True, vmem_limit_bytes=65_700_000
        ),
    )(*flat, cell_valid)
    return tuple(x.reshape(queries.shape) for x in results)


def solution(mesh):
    mesh_sizes = tuple(mesh.shape[name] for name in ("tp", "sy", "sx"))
    spec = P("tp", None, "sy", "sx", None)
    return jax.shard_map(
        functools.partial(local, mesh_sizes),
        mesh=mesh,
        in_specs=(spec, spec, spec, spec, P()),
        out_specs=(spec, spec, spec),
        check_vma=False,
    )
```

time: 556 us -> 81.7 us (0.15)
  the two profiles are of different devices: /device:TPU:26 before, /device:TPU:3 now
where the time goes in v1:
time: 81.7 us
  Pallas kernels  78.8 us (96%)
  local copies, waits for them, and re-layouts  2.24 us (3%)
    pallas_call x1, Pallas kernels, local(): pl.pallas_call(functools.partial(kernel, sizes), name='window_backward',...  78.8 us
    unnamed x3, local copies, waits for them, and re-layouts  2.24 us

profile of v1, /device:TPU:3, one launch (start us, length us, event | category | flops | bytes accessed | tf_op | source)
XLA Modules:
  0.0 81.7 jit_solution(8450221806090625040)
XLA Ops:
  0.6 78.8 %window_backward.1 = (bf16[6,256,128]{2,1,0:T(8,128)(2,1)S(1)}, bf16[6,256,128]{2,1,0:T(8,128)(2,1)S(1)}, bf16[6,256,128]{2,1,0:T(8,128)(2,1)S(1)}) custom-call(bf16[6,256,128]{2,1,0:T(8,128)(2,1)} %bitcast.10, bf16[6,256,128]{2,1,0:T(8,128)(2,1)} %bitcast.11, bf16[6,256,128]{2,1,0:T(8,128)(2,1)} %bitcast.12, bf16[6,256,128]{2,1,0:T(8,128)(2,1)} %bitcast.13, ...), custom_call_target="tpu_custom_call" | custom-call | tf_op jit(solution)/shard_map/window_backward/pallas_call | solution.py:432
  79.4 0.7 copy.11
  80.2 0.7 copy.12
  80.9 0.7 copy.13
